TPU v7x, 256 devices: a whole 4x4x8 slice. The times are simulated.
256 devices in a mesh: rep: 8 (over z_lo, x), exp: 32 (over y, z_hi, core).
Axes of the slice: x: 4, y: 4, z: 8 (z_hi: 4, z_lo: 2; z = z_hi * 2 + z_lo), core: 2. Of those that a mesh axis runs over, the one named last changes fastest.
Arguments:
- hidden: bfloat16 [4096, 7168], P(('rep', 'exp')), may hold values from -6 to 6
- expert_ids: int32 [4096, 8], P(('rep', 'exp')), may hold values from 0 to 15, all different within a row; in each aligned block of 16 rows (0 to 15, 16 to 31, ...) at most 10 rows name the same one
- router: bfloat16 [7168, 16], replicated, may hold values from -0.0625 to 0.0625
- gate_up: bfloat16 [32, 512, 2, 7168], P('exp', 'rep'), may hold values from -0.0625 to 0.0625
- down_weight: bfloat16 [32, 512, 7168], P('exp', 'rep'), may hold values from -0.1875 to 0.1875
- query_latent: bfloat16 [4096, 64, 512], P(('rep', 'exp')), may hold values from -110 to 110
- query_rope: bfloat16 [4096, 64, 64], P(('rep', 'exp')), may hold values from -6 to 6
- cache_latent: bfloat16 [4096, 256, 512], P(('rep', 'exp')), may hold values from -8 to 8
- cache_rope: bfloat16 [4096, 64, 256], P(('rep', 'exp')), may hold values from -5 to 5
- lengths: int32 [4096], P(('rep', 'exp')), may hold values from 32 to 256, as said below
Outputs:
- moe_out: bfloat16 [4096, 7168], P(('rep', 'exp'))
- attn_latent: bfloat16 [4096, 64, 512], P(('rep', 'exp'))
Inputs may be any that keep to these rules, and one draw needn't show every extreme that they name: `expert_ids`: in every aligned block of 16 rows no expert is named by more than 10 pairs, a bound that some block reaches. `lengths`: some row has length 256.
All inputs are finite; a program needn't handle non-finite values.
Results may differ from a plain program's by a relative error of at most 0.015.
Values may be sent and summed in bfloat16 or wider, within the bound.
No kernel may reach another device: no remote copies, remote signals or barrier semaphores. Data moves between devices by JAX's collectives and lax.ppermute only.
A program may use at most 128 MiB of HBM per device.

v0:
```python
import math
import jax
import jax.numpy as jnp
from jax import lax
from jax.sharding import PartitionSpec as P

ROPE = 64
NOPE = 128
route_scale = 2.827


def slot_table(expert_ids, experts, capacity):
    flat_ids = expert_ids.reshape(-1)
    onehot = (flat_ids[:, None] == jnp.arange(experts, dtype=jnp.int32)[None, :]).astype(jnp.int32)
    earlier = jnp.cumsum(onehot, axis=0) - onehot
    slot_rank = jnp.sum(earlier * onehot, axis=1)
    return flat_ids * capacity + slot_rank


def bucket_rows(rows_in, flat_slot, experts, capacity):
    row_total = rows_in.shape[0]
    pair_total = flat_slot.shape[0]
    slot_matrix = (
        jnp.arange(experts * capacity, dtype=jnp.int32)[:, None] == flat_slot[None, :]
    ).astype(jnp.float32)
    slot_matrix = jnp.sum(
        slot_matrix.reshape(experts * capacity, row_total, pair_total // row_total), axis=2
    )
    return jnp.dot(
        slot_matrix.astype(jnp.bfloat16), rows_in, preferred_element_type=jnp.float32
    ).astype(jnp.bfloat16)


def partial_output(rows_in, gate_up, down_weight):
    dims = (((1,), (1,)), ((), ()))
    gate_value = lax.dot_general(
        rows_in, gate_up[:, 0, :], dims, preferred_element_type=jnp.float32
    )
    up_value = lax.dot_general(rows_in, gate_up[:, 1, :], dims, preferred_element_type=jnp.float32)
    activated = (jax.nn.silu(gate_value) * up_value).astype(jnp.bfloat16)
    return jnp.dot(activated, down_weight, preferred_element_type=jnp.float32)


def attend(query_latent, query_rope, cache_latent, cache_rope, row_lengths):
    score_scale = 1.0 / math.sqrt(NOPE + ROPE)
    scores = jnp.einsum(
        "rhc,rlc->rhl", query_latent, cache_latent, preferred_element_type=jnp.float32
    )
    scores = scores + jnp.einsum(
        "rhp,rpl->rhl", query_rope, cache_rope, preferred_element_type=jnp.float32
    )
    scores = scores * score_scale
    valid_mask = (
        jnp.arange(cache_latent.shape[1], dtype=jnp.int32)[None, None, :]
        < row_lengths[:, None, None]
    )
    scores = jnp.where(valid_mask, scores, -1e30)
    row_max = jnp.max(scores, axis=2, keepdims=True)
    weights_raw = jnp.where(valid_mask, jnp.exp(scores - row_max), 0.0)
    attn_probs = (weights_raw / jnp.sum(weights_raw, axis=2, keepdims=True)).astype(jnp.bfloat16)
    output = jnp.einsum(
        "rhl,rlc->rhc", attn_probs, cache_latent, preferred_element_type=jnp.float32
    )
    return output.astype(jnp.bfloat16)


def on_device(
    hidden,
    expert_ids,
    router,
    gate_up,
    down_weight,
    query_latent,
    query_rope,
    cache_latent,
    cache_rope,
    lengths,
):
    groups = lax.axis_size("exp")
    experts = groups // 2
    rows_dev = hidden.shape[0]
    top_k = expert_ids.shape[1]
    model_width = hidden.shape[1]
    capacity = min(rows_dev, max(2, rows_dev * top_k * 5 // (4 * experts)))
    full_gate_up, full_down = (
        lax.all_gather(gate_up, "rep", axis=1, tiled=True),
        lax.all_gather(down_weight, "rep", axis=1, tiled=True),
    )
    slice_gate_up = full_gate_up[0]
    slice_down = full_down[0]
    logits = jnp.dot(hidden, router, preferred_element_type=jnp.float32)
    onehot = (expert_ids[:, :, None] == jnp.arange(experts, dtype=jnp.int32)[None, None, :]).astype(
        jnp.float32
    )
    picked = jnp.sum(onehot * logits[:, None, :], axis=2)
    sigmoid_scores = jax.nn.sigmoid(picked)
    mixing = sigmoid_scores / jnp.sum(sigmoid_scores, axis=1, keepdims=True) * route_scale
    flat_slot = slot_table(expert_ids, experts, capacity)
    buckets = bucket_rows(hidden, flat_slot, experts, capacity).reshape(
        experts, capacity, model_width
    )
    outgoing = jnp.broadcast_to(buckets[:, None], (experts, 2, capacity, model_width)).reshape(
        groups, capacity, model_width
    )
    arrived = lax.all_to_all(outgoing, "exp", split_axis=0, concat_axis=0, tiled=True)
    item_total = arrived.shape[1]
    slice_parts = (
        partial_output(arrived.reshape(-1, model_width), slice_gate_up, slice_down)
        .astype(jnp.bfloat16)
        .reshape(groups, item_total, model_width)
    )
    returned = lax.all_to_all(slice_parts, "exp", split_axis=0, concat_axis=0, tiled=True)
    paired = returned.reshape(experts, 2, capacity, model_width).astype(jnp.float32)
    answers = (paired[:, 0] + paired[:, 1]).astype(jnp.bfloat16)
    flat_answers = answers.reshape(experts * capacity, model_width)
    chosen = jnp.take(flat_answers, flat_slot, axis=0).reshape(rows_dev, top_k, model_width)
    moe_out = jnp.sum(chosen.astype(jnp.float32) * mixing[:, :, None], axis=1).astype(jnp.bfloat16)
    attn_latent = attend(query_latent, query_rope, cache_latent, cache_rope, lengths)
    return (moe_out, attn_latent)


def solution(mesh):
    return jax.shard_map(
        on_device,
        mesh=mesh,
        in_specs=(
            P(("rep", "exp"), None),
            P(("rep", "exp"), None),
            P(),
            P("exp", "rep", None, None),
            P("exp", "rep", None),
            P(("rep", "exp"), None, None),
            P(("rep", "exp"), None, None),
            P(("rep", "exp"), None, None),
            P(("rep", "exp"), None, None),
            P(("rep", "exp")),
        ),
        out_specs=(P(("rep", "exp"), None), P(("rep", "exp"), None, None)),
        check_vma=False,
    )
```

profile of v0, /device:TPU:33, one launch (start us, length us, event | category | flops | bytes accessed | tf_op | source)
XLA Modules:
  0.0 641.1 jit_solution(8945141382381900328)
XLA Ops:
  7.2 3.2 copy.25
  10.5 0.7 all-gather.5.cloned.1.call-update
  12.1 1.7 convolution_convert_fusion.1
  13.8 2.8 broadcast_in_dim.48
  16.5 2.9 broadcast_in_dim.49
  19.5 254.0 %all_to_all.10 = bf16[32,10,7168]{2,1,0:T(8,128)(2,1)} all-to-all(bf16[32,10,7168]{2,1,0:T(8,128)(2,1)S(1)} %bitcast.54), channel_id=1, replica_groups=mesh['rep'=8,'exp'=32] {'exp'}, dimensions={0} | all-to-all | bytes 9175040 | tf_op jit(solution)/shard_map/all_to_all | solution.py:105
  273.5 8.1 %reshape.135 = bf16[320,7168]{1,0:T(8,128)(2,1)} reshape(bf16[32,10,7168]{2,1,0:T(8,128)(2,1)} %all_to_all.10) | data formatting | bytes 9175040 | tf_op jit(solution)/shard_map/reshape | solution.py:108
  281.6 41.4 %all-gather.3.cloned.1.call-done = bf16[1,512,2,7168]{3,1,2,0:T(8,128)(2,1)} async-done(((bf16[1,64,2,7168]{3,1,2,0:T(8,128)(2,1)}), bf16[1,512,2,7168]{3,1,2,0:T(8,128)(2,1)}) %all-gather.3.cloned.1.call-update) | async-done | bytes 14680080 | tf_op jit(solution)/shard_map/all_gather | solution.py:86
  322.9 7.0 %fusion.4 = f32[320,512]{1,0:T(8,128)S(1)} fusion(bf16[320,7168]{1,0:T(8,128)(2,1)} %reshape.135, bf16[512,2,7168]{2,0,1:T(8,128)(2,1)} %bitcast.55), kind=kOutput, calls=%fused_computation.11 | convolution fusion | flops 2348810240 | bytes 12582912 | tf_op jit(solution)/shard_map/dot_general | solution.py:36
  330.0 77.4 %all-gather.5.cloned.1.call-done = bf16[1,512,7168]{2,1,0:T(8,128)(2,1)} async-done(((bf16[1,64,7168]{2,1,0:T(8,128)(2,1)}), bf16[1,512,7168]{2,1,0:T(8,128)(2,1)}) %all-gather.5.cloned.1.call-update) | async-done | bytes 7340048 | tf_op jit(solution)/shard_map/all_gather | solution.py:87
  407.4 13.7 %convolution_convert_fusion = bf16[320,7168]{1,0:T(8,128)(2,1)} fusion(bf16[1,512,7168]{2,1,0:T(8,128)(2,1)} %all-gather.5.cloned.1.call-done, bf16[320,7168]{1,0:T(8,128)(2,1)} %reshape.135, bf16[512,2,7168]{2,0,1:T(8,128)(2,1)} %bitcast.56, f32[320,512]{1,0:T(8,128)S(1)} %fusion.4), kind=kOutput, calls=%fused_computation.2 | convolution fusion | flops 4700897280 | bytes 24510464 | tf_op jit(solution)/shard_map/dot_general | solution.py:41
  421.1 7.8 %reshape.136 = bf16[32,10,7168]{2,1,0:T(8,128)(2,1)} reshape(bf16[320,7168]{1,0:T(8,128)(2,1)} %convolution_convert_fusion) | data formatting | bytes 9175040 | tf_op jit(solution)/shard_map/reshape | solution.py:110
  428.9 10.5 %all-to-all-start.1 = ((bf16[32,10,7168]{2,1,0:T(8,128)(2,1)}), bf16[32,10,7168]{2,1,0:T(8,128)(2,1)}, u32[]{:S(2)}, u32[]{:S(2)}) async-start(bf16[32,10,7168]{2,1,0:T(8,128)(2,1)} %reshape.136), calls=%async_computation.1 | async-start | bytes 14680064 | tf_op jit(solution)/shard_map/all_to_all | solution.py:112
  439.6 0.2 fusion.29
  440.2 3.6 fusion.30
  443.7 0.3 fusion.10
  444.0 0.4 fusion.28
  444.5 5.1 convolution_convert_fusion.2
  449.6 156.9 %all-to-all-done.1 = bf16[32,10,7168]{2,1,0:T(8,128)(2,1)} async-done(((bf16[32,10,7168]{2,1,0:T(8,128)(2,1)}), bf16[32,10,7168]{2,1,0:T(8,128)(2,1)}, u32[]{:S(2)}, u32[]{:S(2)}) %all-to-all-start.1) | async-done | bytes 4587552 | tf_op jit(solution)/shard_map/all_to_all | solution.py:112
  606.5 10.2 %convert.1 = f32[16,2,10,7168]{3,2,1,0:T(8,128)} convert(bf16[16,2,10,7168]{3,2,1,0:T(8,128)(2,1)} %bitcast.6) | non-fusion elementwise | flops 2293760 | bytes 13762560 | tf_op jit(solution)/shard_map/convert_element_type | solution.py:113
  616.7 7.9 %fusion.2 = bf16[16,1,10,7168]{3,2,0,1:T(8,128)(2,1)} fusion(f32[16,2,10,7168]{3,2,1,0:T(8,128)} %convert.1), kind=kLoop, calls=%fused_computation.6 | loop fusion | flops 2293760 | bytes 11468800 | tf_op jit(solution)/shard_map/convert_element_type | solution.py:114
  624.6 3.2 convert_element_type.54
  627.8 3.0 gather_fusion
  630.7 3.6 multiply_reduce_fusion
  (33 shorter events, 1.5 us)
Async XLA Ops:
  7.2 433.0 %copy-start = (bf16[16,64,512]{2,1,0:T(8,128)(2,1)S(1)}, bf16[16,64,512]{2,1,0:T(8,128)(2,1)}, u32[]{:S(2)}) copy-start(bf16[16,64,512]{2,1,0:T(8,128)(2,1)} %param.15) | copy-start | bytes 3145732
  7.2 4.0 copy-start.5
  7.2 315.7 %all-gather.3.cloned.1.call-start = ((), (), s32[]{:S(2)}) async-start(), calls=%async_computation.2 | async-start | bytes 16515072 | tf_op jit(solution)/shard_map/all_gather | solution.py:86
  10.4 397.0 %all-gather.5.cloned.1.call-start = ((), (), s32[]{:S(2)}) async-start(), calls=%async_computation.3 | async-start | bytes 8257536 | tf_op jit(solution)/shard_map/all_gather | solution.py:87
  428.9 10.7 %copy-start.1 = (bf16[16,7168]{1,0:T(8,128)(2,1)S(1)}, bf16[16,7168]{1,0:T(8,128)(2,1)}, u32[]{:S(2)}) copy-start(bf16[16,7168]{1,0:T(8,128)(2,1)} %param.10) | copy-start | bytes 688132
  428.9 10.7 %copy-start.4 = (bf16[7168,16]{0,1:T(8,128)(2,1)S(1)}, bf16[7168,16]{0,1:T(8,128)(2,1)}, u32[]{:S(2)}) copy-start(bf16[7168,16]{0,1:T(8,128)(2,1)} %param.12) | copy-start | bytes 688132
  428.9 11.2 %copy-start.6 = (s32[16]{0:T(128)S(1)}, s32[16]{0:T(128)}, u32[]{:S(2)}) copy-start(s32[16]{0:T(128)} %param.19) | copy-start | bytes 196
  428.9 177.6 %all-to-all-start.1 = ((bf16[32,10,7168]{2,1,0:T(8,128)(2,1)}), bf16[32,10,7168]{2,1,0:T(8,128)(2,1)}, u32[]{:S(2)}, u32[]{:S(2)}) async-start(bf16[32,10,7168]{2,1,0:T(8,128)(2,1)} %reshape.136), calls=%async_computation.1 | async-start | bytes 14680064 | tf_op jit(solution)/shard_map/all_to_all | solution.py:112
  439.4 4.3 copy-start.2
  439.4 4.3 copy-start.3
Sparse Core Ops, SparseCore 0:
  10.6 312.3 all-gather.2
  324.7 82.6 all-gather.4
where the time goes:
time: 642 us; the launch traced here: 641 us
  waiting for transfers between devices  276 us (43%)
  blocking collectives  254 us (40%)
  matrix products  31.6 us (5%)
  local copies, waits for them, and re-layouts  31.3 us (5%)
  other arithmetic  23.1 us (4%)
  between operations  14.2 us (2%)
  starting transfers between devices  10.6 us (2%)
    all_to_all x1, blocking collectives, on_device(): lax.all_to_all(outgoing, 'exp', split_axis=0, concat_axis=0, tiled=True)  254 us
    all_to_all x1, waiting for transfers between devices, on_device(): lax.all_to_all(slice_parts, 'exp', split_axis=0, concat_axis=0, tiled=True)  157 us
    all_gather x1, waiting for transfers between devices, on_device(): lax.all_gather(down_weight, 'rep', axis=1, tiled=True)  77.4 us
    all_gather x1, waiting for transfers between devices, on_device(): lax.all_gather(gate_up, 'rep', axis=1, tiled=True)  41.4 us
    dot_general x1, matrix products, partial_output(): return jnp.dot(activated, down_weight, preferred_element_type=jnp.float32)  13.7 us
  transfers between devices with their start and end apart: 3, of which 3 were waited for; matrix products, arithmetic and copies ran while one was open for 5% of the time, Pallas kernels for 0%

commit v1 on v0

--- a/solution.py
+++ b/solution.py
@@ -83,7 +83,9 @@
     model_width = hidden.shape[1]
     capacity = min(rows_dev, max(2, rows_dev * top_k * 5 // (4 * experts)))
     full_gate_up, full_down = (
-        lax.all_gather(gate_up, "rep", axis=1, tiled=True),
+        jnp.concatenate(
+            lax.all_to_all(jnp.stack([gate_up] * lax.axis_size("rep")), "rep", 0, 0), axis=1
+        ),
         lax.all_gather(down_weight, "rep", axis=1, tiled=True),
     )
     slice_gate_up = full_gate_up[0]

time: 642 us -> 700 us (1.090)
  waiting for transfers between devices: 276 us -> 545 us
  blocking collectives: 254 us -> 0 us
  starting transfers between devices: 10.6 us -> 31.6 us
  local copies, waits for them, and re-layouts: 31.3 us -> 52.2 us
    all_to_all x0 -> x2, waiting for transfers between devices: none -> 394 us  [the longest x1 231 us: on_device(): lax.all_to_all(jnp.stack([gate_up] * lax.axis_size('rep')), 'rep', 0, 0)]
    all_to_all x1 -> x0, blocking collectives: 254 us -> none  [on_device(): lax.all_to_all(outgoing, 'exp', split_axis=0, concat_axis=0, tiled=True)]
    all_gather x1, waiting for transfers between devices: 77.4 us -> 0.02 us  [on_device(): lax.all_gather(down_weight, 'rep', axis=1, tiled=True)]
    all_gather x1 -> x0, waiting for transfers between devices: 41.4 us -> none  [on_device(): lax.all_gather(gate_up, 'rep', axis=1, tiled=True)]
    all_to_all x0 -> x2, starting transfers between devices: none -> 17 us  [the longest x1 11.1 us: on_device(): lax.all_to_all(outgoing, 'exp', split_axis=0, concat_axis=0, tiled=True)]
    all_to_all x0 -> x1, local copies, waits for them, and re-layouts: none -> 7.9 us  [on_device(): lax.all_to_all(jnp.stack([gate_up] * lax.axis_size('rep')), 'rep', 0, 0)]
    another operation x0 -> x2, local copies, waits for them, and re-layouts: none -> 7.31 us  [the longest x1 5.46 us: on_device(): jnp.stack([gate_up] * lax.axis_size('rep'))]
  transfers between devices with their start and end apart: 3 -> 4, of which waited for: 3 -> 3; matrix products, arithmetic and copies ran while one was open for 5% -> 4% of each run, Pallas kernels for 0% -> 0%
where the time goes in v1:
time: 700 us; the launch traced here: 693 us
  waiting for transfers between devices  545 us (78%)
  local copies, waits for them, and re-layouts  52.2 us (7%)
  starting transfers between devices  31.6 us (5%)
  matrix products  27.3 us (4%)
  other arithmetic  23.1 us (3%)
  between operations  14.2 us (2%)
    all_to_all x1, waiting for transfers between devices, on_device(): lax.all_to_all(jnp.stack([gate_up] * lax.axis_size('rep')), 'rep', 0, 0)  231 us
    all_to_all x1, waiting for transfers between devices, on_device(): lax.all_to_all(outgoing, 'exp', split_axis=0, concat_axis=0, tiled=True)  163 us
    all_to_all x1, waiting for transfers between devices, on_device(): lax.all_to_all(slice_parts, 'exp', split_axis=0, concat_axis=0, tiled=True)  150 us
    all_to_all x1, starting transfers between devices, on_device(): lax.all_to_all(slice_parts, 'exp', split_axis=0, concat_axis=0, tiled=True)  14.6 us
  transfers between devices with their start and end apart: 4, of which 3 were waited for; matrix products, arithmetic and copies ran while one was open for 4% of the time, Pallas kernels for 0%

profile of v1, /device:TPU:33, one launch (start us, length us, event | category | flops | bytes accessed | tf_op | source)
XLA Modules:
  0.0 693.3 jit_solution(10360059915854904918)
XLA Ops:
  8.8 1.7 convolution_convert_fusion.1
  10.5 2.7 broadcast_in_dim.48
  13.3 5.9 broadcast_in_dim.49
  19.2 11.1 %all-to-all-start = ((bf16[32,10,7168]{2,1,0:T(8,128)(2,1)}), bf16[32,10,7168]{2,1,0:T(8,128)(2,1)}, u32[]{:S(2)}, u32[]{:S(2)}) async-start(bf16[32,10,7168]{2,1,0:T(8,128)(2,1)} %bitcast.55), calls=%async_computation | async-start | bytes 14680064 | tf_op jit(solution)/shard_map/all_to_all | solution.py:107
  30.2 1.9 copy.32
  32.1 162.6 %all-to-all-done = bf16[32,10,7168]{2,1,0:T(8,128)(2,1)} async-done(((bf16[32,10,7168]{2,1,0:T(8,128)(2,1)}), bf16[32,10,7168]{2,1,0:T(8,128)(2,1)}, u32[]{:S(2)}, u32[]{:S(2)}) %all-to-all-start) | async-done | bytes 4587552 | tf_op jit(solution)/shard_map/all_to_all | solution.py:107
  194.7 5.5 stack.2
  200.1 5.9 all-to-all-start.1
  206.8 8.1 %reshape.138 = bf16[320,7168]{1,0:T(8,128)(2,1)} reshape(bf16[32,10,7168]{2,1,0:T(8,128)(2,1)} %all-to-all-done) | data formatting | bytes 9175040 | tf_op jit(solution)/shard_map/reshape | solution.py:110
  214.8 231.2 %all-to-all-done.1 = bf16[8,1,64,2,7168]{4,2,3,1,0:T(8,128)(2,1)} async-done(((bf16[8,1,64,2,7168]{4,2,3,1,0:T(8,128)(2,1)}), bf16[8,1,64,2,7168]{4,2,3,1,0:T(8,128)(2,1)}, u32[]{:S(2)}, u32[]{:S(2)}) %all-to-all-start.1) | async-done | bytes 14680096 | tf_op jit(solution)/shard_map/all_to_all | solution.py:87
  446.0 7.9 %copy.33 = bf16[8,1,64,2,7168]{4,2,0,3,1:T(8,128)(2,1)S(1)} copy(bf16[8,1,64,2,7168]{4,2,3,1,0:T(8,128)(2,1)} %all-to-all-done.1) | data formatting | bytes 29360128 | tf_op jit(solution)/shard_map/all_to_all | solution.py:87
  453.9 5.2 copy-done.1
  459.1 2.6 fusion.4
  461.7 13.9 %convolution_convert_fusion = bf16[320,7168]{1,0:T(8,128)(2,1)} fusion(bf16[1,512,7168]{2,1,0:T(8,128)(2,1)} %all-gather.2.cloned.1.call-done, bf16[320,7168]{1,0:T(8,128)(2,1)} %reshape.138, bf16[512,2,7168]{2,0,1:T(8,128)(2,1)} %bitcast.57, f32[320,512]{1,0:T(8,128)S(1)} %fusion.4), kind=kOutput, calls=%fused_computation.2 | convolution fusion | flops 4700897280 | bytes 24510464 | tf_op jit(solution)/shard_map/dot_general | solution.py:41
  475.6 7.8 %reshape.139 = bf16[32,10,7168]{2,1,0:T(8,128)(2,1)} reshape(bf16[320,7168]{1,0:T(8,128)(2,1)} %convolution_convert_fusion) | data formatting | bytes 9175040 | tf_op jit(solution)/shard_map/reshape | solution.py:112
  483.4 14.6 %all-to-all-start.2 = ((bf16[32,10,7168]{2,1,0:T(8,128)(2,1)}), bf16[32,10,7168]{2,1,0:T(8,128)(2,1)}, u32[]{:S(2)}, u32[]{:S(2)}) async-start(bf16[32,10,7168]{2,1,0:T(8,128)(2,1)} %reshape.139), calls=%async_computation.2 | async-start | bytes 14680064 | tf_op jit(solution)/shard_map/all_to_all | solution.py:114
  498.8 3.6 fusion.30
  503.1 5.1 convolution_convert_fusion.2
  508.2 150.4 %all-to-all-done.2 = bf16[32,10,7168]{2,1,0:T(8,128)(2,1)} async-done(((bf16[32,10,7168]{2,1,0:T(8,128)(2,1)}), bf16[32,10,7168]{2,1,0:T(8,128)(2,1)}, u32[]{:S(2)}, u32[]{:S(2)}) %all-to-all-start.2) | async-done | bytes 4587552 | tf_op jit(solution)/shard_map/all_to_all | solution.py:114
  658.7 10.2 %convert.1 = f32[16,2,10,7168]{3,2,1,0:T(8,128)} convert(bf16[16,2,10,7168]{3,2,1,0:T(8,128)(2,1)} %bitcast.7) | non-fusion elementwise | flops 2293760 | bytes 13762560 | tf_op jit(solution)/shard_map/convert_element_type | solution.py:115
  668.9 7.9 %fusion.2 = bf16[16,1,10,7168]{3,2,0,1:T(8,128)(2,1)} fusion(f32[16,2,10,7168]{3,2,1,0:T(8,128)} %convert.1), kind=kLoop, calls=%fused_computation.6 | loop fusion | flops 2293760 | bytes 11468800 | tf_op jit(solution)/shard_map/convert_element_type | solution.py:116
  676.8 3.2 convert_element_type.54
  679.9 3.0 gather_fusion
  682.9 3.6 multiply_reduce_fusion
  (37 shorter events, 3.8 us)
Async XLA Ops:
  7.2 491.6 %copy-start = (bf16[16,64,512]{2,1,0:T(8,128)(2,1)S(1)}, bf16[16,64,512]{2,1,0:T(8,128)(2,1)}, u32[]{:S(2)}) copy-start(bf16[16,64,512]{2,1,0:T(8,128)(2,1)} %param.15) | copy-start | bytes 3145732
  19.2 175.5 %all-to-all-start = ((bf16[32,10,7168]{2,1,0:T(8,128)(2,1)}), bf16[32,10,7168]{2,1,0:T(8,128)(2,1)}, u32[]{:S(2)}, u32[]{:S(2)}) async-start(bf16[32,10,7168]{2,1,0:T(8,128)(2,1)} %bitcast.55), calls=%async_computation | async-start | bytes 14680064 | tf_op jit(solution)/shard_map/all_to_all | solution.py:107
  200.1 245.9 %all-to-all-start.1 = ((bf16[8,1,64,2,7168]{4,2,3,1,0:T(8,128)(2,1)}), bf16[8,1,64,2,7168]{4,2,3,1,0:T(8,128)(2,1)}, u32[]{:S(2)}, u32[]{:S(2)}) async-start(bf16[8,1,64,2,7168]{4,2,3,1,0:T(8,128)(2,1)} %stack.2), calls=%async_computation.1 | async-start | bytes 29360128 | tf_op jit(solution)/shard_map/all_to_all | solution.py:87
  206.1 255.7 %all-gather.2.cloned.1.call-start = ((), (), s32[]{:S(2)}) async-start(), calls=%async_computation.3 | async-start | bytes 8257536 | tf_op jit(solution)/shard_map/all_gather | solution.py:89
  446.0 13.1 %copy-start.2 = (bf16[320,7168]{1,0:T(8,128)(2,1)S(1)}, bf16[320,7168]{1,0:T(8,128)(2,1)}, u32[]{:S(2)}) copy-start(bf16[320,7168]{1,0:T(8,128)(2,1)} %reshape.138) | copy-start | bytes 13762564
  453.9 5.2 copy-start.1
  483.4 14.8 %copy-start.3 = (bf16[16,7168]{1,0:T(8,128)(2,1)S(1)}, bf16[16,7168]{1,0:T(8,128)(2,1)}, u32[]{:S(2)}) copy-start(bf16[16,7168]{1,0:T(8,128)(2,1)} %param.10) | copy-start | bytes 688132
  483.4 14.8 %copy-start.6 = (bf16[7168,16]{0,1:T(8,128)(2,1)S(1)}, bf16[7168,16]{0,1:T(8,128)(2,1)}, u32[]{:S(2)}) copy-start(bf16[7168,16]{0,1:T(8,128)(2,1)} %param.12) | copy-start | bytes 688132
  483.4 15.3 %copy-start.7 = (s32[16]{0:T(128)S(1)}, s32[16]{0:T(128)}, u32[]{:S(2)}) copy-start(s32[16]{0:T(128)} %param.19) | copy-start | bytes 196
  483.4 175.3 %all-to-all-start.2 = ((bf16[32,10,7168]{2,1,0:T(8,128)(2,1)}), bf16[32,10,7168]{2,1,0:T(8,128)(2,1)}, u32[]{:S(2)}, u32[]{:S(2)}) async-start(bf16[32,10,7168]{2,1,0:T(8,128)(2,1)} %reshape.139), calls=%async_computation.2 | async-start | bytes 14680064 | tf_op jit(solution)/shard_map/all_to_all | solution.py:114
  498.0 4.3 copy-start.4
  498.1 4.3 copy-start.5
Sparse Core Ops, SparseCore 0:
  208.7 236.7 all-gather.1
